TPU v7x, 512 devices: a whole 4x8x8 slice. The times are simulated.
512 devices in a mesh: tm: 64 (over z, x, core), band: 8 (over y).
Axes of the slice: x: 4, y: 8, z: 8, core: 2. Of those that a mesh axis runs over, the one named last changes fastest.
Arguments:
- query_input: bfloat16 [64, 40, 26, 1120], P('tm', 'band'), may hold values from -6 to 6
- key_input: bfloat16 [64, 40, 26, 1120], P('tm', 'band'), may hold values from -8 to 8
- value_input: bfloat16 [64, 40, 26, 1120], P('tm', 'band'), may hold values from -12 to 12
- cotangent: bfloat16 [64, 40, 26, 1120], P('tm', 'band'), may hold values from -6 to 6
- local_kernel_weight: float32 [3, 3, 1120], replicated, may hold values from -2 to 2
Outputs:
- mixed_out: bfloat16 [64, 40, 26, 1120], P('tm', 'band')
- query_grad: bfloat16 [64, 40, 26, 1120], P('tm', 'band')
- key_grad: bfloat16 [64, 40, 26, 1120], P('tm', 'band')
- value_grad: bfloat16 [64, 40, 26, 1120], P('tm', 'band')
- kernel_grad: float32 [3, 3, 1120], replicated
All inputs are finite; a program needn't handle non-finite values.
Results may differ from a plain program's by a relative error of at most 0.018.
Values may be sent and summed in bfloat16 or wider, within the bound.
No kernel may reach another device: no remote copies, remote signals or barrier semaphores. Data moves between devices by JAX's collectives and lax.ppermute only.
A program may use at most 128 MiB of HBM per device.

v0:
```python
import math
import jax
import jax.numpy as jnp
from jax import lax
from jax.sharding import PartitionSpec as P

HEADS = 35
HEAD_DIM = 32


def entering(shard, axis, combine, identity, reverse):
    devices, mine = (lax.axis_size(axis), lax.axis_index(axis))
    everything = jax.tree.map(lambda part: lax.all_gather(part, axis), shard)
    start = jax.tree.map(
        lambda part, zero: jnp.broadcast_to(jnp.asarray(zero, part.dtype), part.shape),
        shard,
        identity,
    )

    def step(k, before):
        at = devices - 1 - k if reverse else k
        reached = at > mine if reverse else at < mine
        new = combine(before, jax.tree.map(lambda part: part[at], everything))
        return jax.tree.map(lambda a, b: jnp.where(reached, a, b), new, before)

    return lax.fori_loop(0, devices, step, start)


def padded(cells, sides, width):
    for axis, dim in sides:
        count = lax.axis_size(axis)
        ends = count - 1
        head = lax.slice_in_dim(cells, 0, width, axis=dim)
        tail = lax.slice_in_dim(cells, cells.shape[dim] - width, cells.shape[dim], axis=dim)
        cells = jnp.concatenate(
            [
                lax.ppermute(tail, axis, [(i, (i + 1) % count) for i in range(ends)]),
                cells,
                lax.ppermute(head, axis, [((i + 1) % count, i) for i in range(ends)]),
            ],
            axis=dim,
        )
    return cells


def feature(x):
    return jnp.where(x > 0, x + 1.0, jnp.exp(jnp.minimum(x, 0.0)))


def slope(x):
    return jnp.where(x > 0, jnp.ones_like(x), jnp.exp(jnp.minimum(x, 0.0)))


def add_pair(earlier, later_term):
    return (earlier[0] + later_term[0], earlier[1] + later_term[1])


def frame_totals(terms, backward):
    frame = lax.psum(terms, "band")
    start = (jnp.zeros_like(frame[0]), jnp.zeros_like(frame[1]))
    before = entering(frame, "tm", add_pair, start, backward)
    return add_pair(before, frame)


def group_heads_count():
    chosen = 1
    for candidate in range(1, HEADS + 1):
        if HEADS % candidate == 0 and candidate * HEAD_DIM <= 256:
            chosen = candidate
    return chosen


def block_outer(left, right, group_count, group_heads, precise):
    count = left.shape[0]
    group_width = group_heads * HEAD_DIM
    left_groups = left.reshape(count, group_count, group_width)
    right_groups = right.reshape(count, group_count, group_width)
    if precise:
        whole = jnp.einsum(
            "tga,tgb->gab", left_groups, right_groups, precision=lax.Precision.HIGHEST
        )
    else:
        whole = jnp.einsum(
            "tga,tgb->gab", left_groups, right_groups, preferred_element_type=jnp.float32
        )
    whole = whole.reshape(group_count, group_heads, HEAD_DIM, group_heads, HEAD_DIM)
    same_head = jnp.eye(group_heads, dtype=jnp.float32)[None, :, None, :, None]
    return jnp.sum(whole * same_head, axis=3).reshape(HEADS, HEAD_DIM, HEAD_DIM)


def block_matrix(state, group_count, group_heads):
    group_width = group_heads * HEAD_DIM
    placed = state.reshape(group_count, group_heads, HEAD_DIM, 1, HEAD_DIM)
    same_head = jnp.eye(group_heads, dtype=jnp.float32)[None, :, None, :, None]
    return (placed * same_head).reshape(group_count, group_width, group_width)


def apply_blocks(rows, blocks, transposed):
    count = rows.shape[0]
    group_count, group_width = (blocks.shape[0], blocks.shape[1])
    grouped = rows.reshape(count, group_count, group_width)
    if transposed:
        result = jnp.einsum("tgb,gab->tga", grouped, blocks, precision=lax.Precision.HIGHEST)
    else:
        result = jnp.einsum("tga,gab->tgb", grouped, blocks, precision=lax.Precision.HIGHEST)
    return result.reshape(count, group_count * group_width)


def shards(query_input, key_input, value_input, cotangent, local_kernel_weight):
    high = lax.Precision.HIGHEST
    band_row_span, column_count, width = (
        query_input.shape[1],
        query_input.shape[2],
        query_input.shape[3],
    )
    count = band_row_span * column_count
    group_heads = group_heads_count()
    group_count = HEADS // group_heads
    indicator = (jnp.arange(width)[:, None] // HEAD_DIM == jnp.arange(HEADS)[None, :]).astype(
        jnp.float32
    )
    q_raw = query_input[0].reshape(count, width).astype(jnp.float32)
    k_raw = key_input[0].reshape(count, width).astype(jnp.float32)
    q_feat = feature(q_raw).astype(jnp.bfloat16)
    k_feat = feature(k_raw).astype(jnp.bfloat16)
    value_flat = value_input[0].reshape(count, width)
    own_state = block_outer(k_feat, value_flat, group_count, group_heads, False)
    own_norm = jnp.sum(k_feat, axis=0, dtype=jnp.float32).reshape(HEADS, HEAD_DIM)
    state, norm_vec = frame_totals((own_state, own_norm), False)
    q_wide = q_feat.astype(jnp.float32)
    state_blocks = block_matrix(state, group_count, group_heads)
    norm_flat = norm_vec.reshape(width)
    num = apply_blocks(q_wide, state_blocks, False)
    den = jnp.dot(q_wide * norm_flat, indicator, precision=high)
    den_wide = jnp.dot(den, indicator.T, precision=high)
    attn = num / den_wide
    stacked = jnp.stack([value_input[0], cotangent[0]])
    rimmed = padded(stacked, (("band", 1),), 1)
    padded_input = jnp.pad(rimmed, ((0, 0), (0, 0), (1, 1), (0, 0)))
    value_padded = padded_input[0]
    gpad = padded_input[1]
    complete_gradient = cotangent[0].astype(jnp.float32)
    local_output = jnp.zeros((band_row_span, column_count, width), jnp.float32)
    v_local = jnp.zeros((band_row_span, column_count, width), jnp.float32)
    kernel_row_slice = []
    for row_offset in range(3):
        for column_offset in range(3):
            local_output = (
                local_output
                + local_kernel_weight[row_offset, column_offset]
                * value_padded[
                    row_offset : row_offset + band_row_span,
                    column_offset : column_offset + column_count,
                ]
            )
            v_local = (
                v_local
                + local_kernel_weight[row_offset, column_offset]
                * gpad[
                    2 - row_offset : 2 - row_offset + band_row_span,
                    2 - column_offset : 2 - column_offset + column_count,
                ]
            )
            kernel_row_slice.append(
                jnp.sum(
                    complete_gradient
                    * value_padded[
                        row_offset : row_offset + band_row_span,
                        column_offset : column_offset + column_count,
                    ],
                    axis=(0, 1),
                )
            )
    mixed_out = (attn.reshape(band_row_span, column_count, width) + local_output).astype(
        jnp.bfloat16
    )[None]
    grad_flat = complete_gradient.reshape(count, width)
    scaled = grad_flat / den_wide
    den_grad = -jnp.dot(grad_flat * attn, indicator, precision=high) / den
    den_grad_wide = jnp.dot(den_grad, indicator.T, precision=high)
    back_state = block_outer(q_wide, scaled, group_count, group_heads, True)
    back_norm = jnp.sum(q_wide * den_grad_wide, axis=0).reshape(HEADS, HEAD_DIM)
    later_state, later_norm = frame_totals((back_state, back_norm), True)
    query_grad = apply_blocks(scaled, state_blocks, True) + den_grad_wide * norm_flat
    query_grad = (
        (query_grad * slope(q_raw))
        .reshape(band_row_span, column_count, width)
        .astype(jnp.bfloat16)[None]
    )
    later_blocks = block_matrix(later_state, group_count, group_heads)
    key_grad = apply_blocks(
        value_flat.astype(jnp.float32), later_blocks, True
    ) + later_norm.reshape(width)
    key_grad = (
        (key_grad * slope(k_raw))
        .reshape(band_row_span, column_count, width)
        .astype(jnp.bfloat16)[None]
    )
    value_grad = apply_blocks(k_feat.astype(jnp.float32), later_blocks, False)
    value_grad = (value_grad.reshape(band_row_span, column_count, width) + v_local).astype(
        jnp.bfloat16
    )[None]
    kernel_terms = jnp.stack(kernel_row_slice).reshape(3, 3, width)
    kernel_total = lax.psum(kernel_terms, ("tm", "band"))
    total_tokens = lax.axis_size("tm") * lax.axis_size("band") * count
    kernel_grad = kernel_total / math.sqrt(total_tokens)
    return (mixed_out, query_grad, key_grad, value_grad, kernel_grad)


def solution(mesh):
    placed = (
        P("tm", "band", None, None),
        P("tm", "band", None, None),
        P("tm", "band", None, None),
        P("tm", "band", None, None),
        P(),
    )
    return jax.shard_map(
        shards,
        mesh=mesh,
        in_specs=placed,
        out_specs=(
            P("tm", "band", None, None),
            P("tm", "band", None, None),
            P("tm", "band", None, None),
            P("tm", "band", None, None),
            P(),
        ),
        check_vma=False,
    )
```

profile of v0, /device:TPU:1, one launch (start us, length us, event | category | flops | bytes accessed | tf_op | source)
XLA Modules:
  0.0 863.7 jit_solution(13523367854085724787)
XLA Ops:
  10.0 2.6 reshape.180
  12.5 4.8 multiply_reduce_fusion.1
  17.4 79.9 %all-reduce.4.cloned.1.call-done = f32[35,32,32]{2,1,0:T(8,128)} async-done(((f32[35,32,32]{2,1,0:T(8,128)}), f32[35,32,32]{2,1,0:T(8,128)}) %all-reduce.4.cloned.1.call-update) | async-done | bytes 143376 | tf_op jit(solution)/shard_map/psum | solution.py:59
  97.5 22.3 %psum.36 = f32[35,32]{1,0:T(8,128)S(1)} all-reduce(f32[35,32]{1,0:T(8,128)S(1)} %reshape.182), channel_id=1, replica_groups=mesh['tm'=64,'band'=8] {'band'}, use_global_device_ids=true, to_apply=%region_3.4 | all-reduce | flops 1120 | bytes 8960 | tf_op jit(solution)/shard_map/psum | solution.py:59
  121.4 1.3 select_n.138
  123.8 69.4 %all-gather.4 = f32[64,35,32]{1,2,0:T(8,128)} all-gather(f32[1,35,32]{1,2,0:T(8,128)S(1)} %copy.44), channel_id=3, replica_groups=mesh['tm'=64,'band'=8] {'tm'}, dimensions={0}, use_global_device_ids=true | all-gather | bytes 291200 | tf_op jit(solution)/shard_map/all_gather | solution.py:13
  193.2 69.6 %all-gather.9.cloned.1.call-done = f32[2240,32,32]{2,1,0:T(8,128)} async-done(((f32[35,32,32]{2,1,0:T(8,128)}), f32[2240,32,32]{2,1,0:T(8,128)}) %all-gather.9.cloned.1.call-update) | async-done | bytes 9175056 | tf_op jit(solution)/shard_map/all_gather | solution.py:13
  262.8 135.1 %while.34 = (s32[]{:T(128)}, f32[35,32,32]{2,1,0:T(8,128)S(1)}, f32[35,32]{1,0:T(8,128)S(1)}, s32[]{:T(128)}, f32[64,35,32,32]{3,2,1,0:T(8,128)}, /*index=5*/f32[64,35,32]{1,2,0:T(8,128)}, s32[]{:T(128)}, s32[]{:T(128)}) while((s32[]{:T(128)}, f32[35,32,32]{2,1,0:T(8,128)S(1)}, f32[35,32]{1,0:T(8,128)S(1)}, s32[]{:T(128)}, ...), condition=%wide.region_5.6_spmd.clone, body=%wide.region_4.5_spmd.clone.sunk | while | flops 110884 | bytes 461555 | solution.py:26
  262.8 1.3 add_select_fusion.9
  264.9 1.3 add_select_fusion.9
  267.1 1.3 add_select_fusion.9
  269.2 1.3 add_select_fusion.9
  271.3 1.3 add_select_fusion.9
  273.4 1.3 add_select_fusion.9
  275.5 1.3 add_select_fusion.9
  277.6 1.3 add_select_fusion.9
  279.7 1.3 add_select_fusion.9
  281.8 1.3 add_select_fusion.9
  283.9 1.3 add_select_fusion.9
  286.0 1.3 add_select_fusion.9
  288.1 1.3 add_select_fusion.9
  290.3 1.3 add_select_fusion.9
  292.4 1.3 add_select_fusion.9
  294.5 1.3 add_select_fusion.9
  296.6 1.3 add_select_fusion.9
  298.7 1.3 add_select_fusion.9
  300.8 1.3 add_select_fusion.9
  302.9 1.3 add_select_fusion.9
  305.0 1.3 add_select_fusion.9
  307.1 1.3 add_select_fusion.9
  309.2 1.3 add_select_fusion.9
  311.4 1.3 add_select_fusion.9
  313.5 1.3 add_select_fusion.9
  315.6 1.3 add_select_fusion.9
  317.7 1.3 add_select_fusion.9
  319.8 1.3 add_select_fusion.9
  321.9 1.3 add_select_fusion.9
  398.0 2.4 mul.264
  400.4 3.6 mul.265
  405.9 2.4 reshape.183
  409.2 3.0 fusion.73
  412.2 1.5 reshape.185
  413.7 2.0 fusion.49
  415.7 3.9 reshape.187
  419.6 4.8 multiply_reduce_fusion
  424.4 70.0 %all-reduce.6.cloned.1.call-done = f32[35,32,32]{2,1,0:T(8,128)} async-done(((f32[35,32,32]{2,1,0:T(8,128)}), f32[35,32,32]{2,1,0:T(8,128)}) %all-reduce.6.cloned.1.call-update) | async-done | bytes 143376 | tf_op jit(solution)/shard_map/psum | solution.py:59
  494.6 3.2 collective-permute-start
  497.8 1.5 collective-permute-start.1
  499.3 2.0 select_n.142
  501.4 2.2 collective-permute-done.1
  503.6 1.5 fusion.10
  506.2 107.4 %psum.39 = f32[3,3,1120]{2,1,0:T(4,128)S(1)} all-reduce(f32[3,3,1120]{2,1,0:T(4,128)S(1)} %reshape.191), channel_id=1, replica_groups=mesh['tm'=64,'band'=8] {'tm','band'}, use_global_device_ids=true, to_apply=%region_21.22 | all-reduce | flops 10080 | bytes 80640 | tf_op jit(solution)/shard_map/psum | solution.py:204
  614.3 3.1 convolution_bitcast_fusion.3
  618.8 2.1 reshape.184
  620.9 2.2 fusion.4
  624.0 24.1 %psum.38 = f32[35,32]{1,0:T(8,128)S(1)} all-reduce(f32[35,32]{1,0:T(8,128)S(1)} %reshape.189), channel_id=1, replica_groups=mesh['tm'=64,'band'=8] {'band'}, use_global_device_ids=true, to_apply=%region_9.10 | all-reduce | flops 1120 | bytes 8960 | tf_op jit(solution)/shard_map/psum | solution.py:59
  649.0 58.1 %all-gather.5 = f32[64,35,32]{1,2,0:T(8,128)} all-gather(f32[1,35,32]{1,2,0:T(8,128)S(1)} %copy.52), channel_id=5, replica_groups=mesh['tm'=64,'band'=8] {'tm'}, dimensions={0}, use_global_device_ids=true | all-gather | bytes 291200 | tf_op jit(solution)/shard_map/all_gather | solution.py:13
  707.0 1.4 fusion.52
  708.4 135.5 %while.35 = (s32[]{:T(128)}, f32[35,32,32]{2,1,0:T(8,128)S(1)}, f32[35,32]{1,0:T(8,128)S(1)}, s32[]{:T(128)}, f32[64,35,32,32]{3,2,1,0:T(8,128)}, /*index=5*/f32...) while((s32[]{:T(128)}, f32[35,32,32]{2,1,0:T(8,128)S(1)}, ...), condition=%wide.region_11.12_spmd.clone, body=%wide.region_10.11_spmd.clone.sunk | while | flops 110888 | bytes 461617 | solution.py:26
  708.4 1.3 add_select_fusion.11
  844.0 2.4 mul.306
  846.4 3.6 mul.307
  851.1 1.8 convolution_bitcast_fusion.1
  854.8 1.4 fusion.53
  (592 shorter events, 246.8 us)
Async XLA Ops:
  7.2 1.8 copy-start.17
  7.2 90.1 %all-reduce.4.cloned.1.call-start = ((), (), s32[]{:S(2)}) async-start(), calls=%async_computation | async-start | bytes 1146880 | tf_op jit(solution)/shard_map/psum | solution.py:59
  9.0 1.0 copy-start.5
  9.5 3.0 copy-start.7
  17.4 245.4 %all-gather.9.cloned.1.call-start = ((), (), s32[]{:S(2)}) async-start(), calls=%async_computation.2 | async-start | bytes 37273600 | tf_op jit(solution)/shard_map/all_gather | solution.py:13
  97.3 22.9 %copy-start.20 = (bf16[1,5,26,1120]{3,2,1,0:T(8,128)(2,1)S(1)}, bf16[1,5,26,1120]{3,2,1,0:T(8,128)(2,1)}, u32[]{:S(2)}) copy-start(bf16[1,5,26,1120]{3,2,1,0:T(8,128)(2,1)} %param.9) | copy-start | bytes 873604
  97.3 397.1 %all-reduce.6.cloned.1.call-start = ((), (), s32[]{:S(2)}) async-start(), calls=%async_computation.1 | async-start | bytes 1146880 | tf_op jit(solution)/shard_map/psum | solution.py:59
  121.4 1.4 copy-start.3
  122.7 285.6 %copy-start.1 = (f32[130,1120]{1,0:T(8,128)}, f32[130,1120]{1,0:T(8,128)S(1)}, u32[]{:S(2)}) copy-start(f32[130,1120]{1,0:T(8,128)S(1)} %reshape.192) | copy-start | bytes 1747204
  262.8 135.1 %copy-start.16 = (f32[35,32,32]{2,1,0:T(8,128)S(1)}, f32[35,32,32]{2,1,0:T(8,128)}, u32[]{:S(2)}) copy-start(f32[35,32,32]{2,1,0:T(8,128)} %all-reduce.4.cloned.1.call-done) | copy-start | bytes 430084
  400.4 3.6 copy-start.9
  412.2 1.5 copy-start.10
  413.7 5.8 copy-start
  424.4 70.1 %copy-start.18 = (bf16[1,5,26,1120]{3,2,1,0:T(8,128)(2,1)S(1)}, bf16[1,5,26,1120]{3,2,1,0:T(8,128)(2,1)}, u32[]{:S(2)}) copy-start(bf16[1,5,26,1120]{3,2,1,0:T(8,128)(2,1)} %param.11) | copy-start | bytes 873604
  424.4 284.0 %all-gather.11.cloned.1.call-start = ((), (), s32[]{:S(2)}) async-start(), calls=%async_computation.3 | async-start | bytes 37273600 | tf_op jit(solution)/shard_map/all_gather | solution.py:13
  494.5 3.2 copy-start.12
  494.5 6.8 copy-start.21
  494.6 6.9 collective-permute-start
  497.8 5.9 collective-permute-start.1
  618.8 4.3 copy-start.2
  620.9 2.2 copy-start.13
  620.9 2.2 copy-start.14
  623.9 83.1 %copy-start.4 = (f32[5,26,1120]{2,1,0:T(8,128)S(1)}, f32[5,26,1120]{2,1,0:T(8,128)}, u32[]{:S(2)}) copy-start(f32[5,26,1120]{2,1,0:T(8,128)} %reshape.184) | copy-start | bytes 1747204
  708.4 135.5 %copy-start.15 = (f32[35,32,32]{2,1,0:T(8,128)S(1)}, f32[35,32,32]{2,1,0:T(8,128)}, u32[]{:S(2)}) copy-start(f32[35,32,32]{2,1,0:T(8,128)} %all-reduce.6.cloned.1.call-done) | copy-start | bytes 430084
  846.4 3.6 copy-start.6
  850.0 1.0 copy-start.8
  853.1 1.1 copy-start.11
  854.8 1.4 copy-start.19
Sparse Core Ops, SparseCore 0:
  17.5 79.7 all-reduce.3
  100.6 162.1 all-gather.8
  424.5 69.8 all-reduce.5
  497.6 161.7 all-gather.10
where the time goes:
time: 877 us; the launch traced here: 864 us
  blocking collectives  281 us (32%)
  waiting for transfers between devices  222 us (25%)
  other arithmetic  182 us (21%)
  local copies, waits for them, and re-layouts  141 us (16%)
  matrix products  15.3 us (2%)
  between operations  14.3 us (2%)
    select_n x256, other arithmetic, step(): return jax.tree.map(lambda a, b: jnp.where(reached, a, b), new, before)  163 us
    psum x2, waiting for transfers between devices, frame_totals(): frame = lax.psum(terms, 'band')  150 us
    all_gather x2, blocking collectives, entering(): everything = jax.tree.map(lambda part: lax.all_gather(part, axis), shard)  127 us
    psum x1, blocking collectives, shards(): kernel_total = lax.psum(kernel_terms, ('tm', 'band'))  107 us
    dynamic_slice x256, local copies, waits for them, and re-layouts, step(): new = combine(before, jax.tree.map(lambda part: part[at], everything))  104 us
    all_gather x2, waiting for transfers between devices, entering(): everything = jax.tree.map(lambda part: lax.all_gather(part, axis), shard)  69.6 us
    psum x2, blocking collectives, frame_totals(): frame = lax.psum(terms, 'band')  46.4 us
  transfers between devices with their start and end apart: 6, of which 4 were waited for; matrix products, arithmetic and copies ran while one was open for 2% of the time, Pallas kernels for 0%

commit v1 on v0

--- a/solution.py
+++ b/solution.py
@@ -3,6 +3,7 @@
 import jax.numpy as jnp
 from jax import lax
 from jax.sharding import PartitionSpec as P
+from jax.lax import psum
 
 HEADS = 35
 HEAD_DIM = 32
@@ -201,7 +202,9 @@
         jnp.bfloat16
     )[None]
     kernel_terms = jnp.stack(kernel_row_slice).reshape(3, 3, width)
-    kernel_total = lax.psum(kernel_terms, ("tm", "band"))
+    kernel_total = kernel_terms
+    for dev in ("tm", "band"):
+        kernel_total = psum(kernel_total, dev)
     total_tokens = lax.axis_size("tm") * lax.axis_size("band") * count
     kernel_grad = kernel_total / math.sqrt(total_tokens)
     return (mixed_out, query_grad, key_grad, value_grad, kernel_grad)

time: 877 us -> 1030 us (1.17)
  blocking collectives: 281 us -> 432 us
    psum x1, blocking collectives: 107 us -> 250 us  [shards(): kernel_total = psum(kernel_total, dev)]
  transfers between devices with their start and end apart: 6 -> 6, of which waited for: 4 -> 3; matrix products, arithmetic and copies ran while one was open for 2% -> 2% of each run, Pallas kernels for 0% -> 0%
where the time goes in v1:
time: 1030 us; the launch traced here: 1020 us
  blocking collectives  432 us (42%)
  waiting for transfers between devices  219 us (21%)
  other arithmetic  181 us (18%)
  local copies, waits for them, and re-layouts  145 us (14%)
  matrix products  15 us (1%)
  between operations  14.3 us (1%)
    psum x1, blocking collectives, shards(): kernel_total = psum(kernel_total, dev)  250 us
    select_n x256, other arithmetic, step(): return jax.tree.map(lambda a, b: jnp.where(reached, a, b), new, before)  163 us
    psum x2, waiting for transfers between devices, frame_totals(): frame = lax.psum(terms, 'band')  150 us
    all_gather x2, blocking collectives, entering(): everything = jax.tree.map(lambda part: lax.all_gather(part, axis), shard)  135 us
    dynamic_slice x256, local copies, waits for them, and re-layouts, step(): new = combine(before, jax.tree.map(lambda part: part[at], everything))  104 us
    all_gather x2, waiting for transfers between devices, entering(): everything = jax.tree.map(lambda part: lax.all_gather(part, axis), shard)  69.6 us
    psum x2, blocking collectives, frame_totals(): frame = lax.psum(terms, 'band')  46.4 us
  transfers between devices with their start and end apart: 6, of which 3 were waited for; matrix products, arithmetic and copies ran while one was open for 2% of the time, Pallas kernels for 0%

profile of v1, /device:TPU:1, one launch (start us, length us, event | category | flops | bytes accessed | tf_op | source)
XLA Modules:
  0.0 1016.0 jit_solution(2246477865476165636)
XLA Ops:
  7.2 1.5 reshape_reshape_squeeze.3
  10.0 2.6 reshape.180
  12.5 4.8 multiply_reduce_fusion.1
  17.4 79.9 %all-reduce.5.cloned.1.call-done = f32[35,32,32]{2,1,0:T(8,128)} async-done(((f32[35,32,32]{2,1,0:T(8,128)}), f32[35,32,32]{2,1,0:T(8,128)}) %all-reduce.5.cloned.1.call-update) | async-done | bytes 143376 | tf_op jit(solution)/shard_map/psum | solution.py:60
  98.4 22.5 %psum.43 = f32[35,32]{1,0:T(8,128)S(1)} all-reduce(f32[35,32]{1,0:T(8,128)S(1)} %reshape.182), channel_id=1, replica_groups=mesh['tm'=64,'band'=8] {'band'}, use_global_device_ids=true, to_apply=%region_3.4 | all-reduce | flops 1120 | bytes 8960 | tf_op jit(solution)/shard_map/psum | solution.py:60
  122.4 1.3 select_n.138
  123.8 69.4 %all-gather.4 = f32[64,35,32]{1,2,0:T(8,128)} all-gather(f32[1,35,32]{1,2,0:T(8,128)S(1)} %copy.44), channel_id=3, replica_groups=mesh['tm'=64,'band'=8] {'tm'}, dimensions={0}, use_global_device_ids=true | all-gather | bytes 291200 | tf_op jit(solution)/shard_map/all_gather | solution.py:14
  193.2 69.6 %all-gather.9.cloned.1.call-done = f32[2240,32,32]{2,1,0:T(8,128)} async-done(((f32[35,32,32]{2,1,0:T(8,128)}), f32[2240,32,32]{2,1,0:T(8,128)}) %all-gather.9.cloned.1.call-update) | async-done | bytes 9175056 | tf_op jit(solution)/shard_map/all_gather | solution.py:14
  262.7 135.1 %while.34 = (s32[]{:T(128)}, f32[35,32,32]{2,1,0:T(8,128)S(1)}, f32[35,32]{1,0:T(8,128)S(1)}, s32[]{:T(128)}, f32[64,35,32,32]{3,2,1,0:T(8,128)}, /*index=5*/f32[64,35,32]{1,2,0:T(8,128)}, s32[]{:T(128)}, s32[]{:T(128)}) while((s32[]{:T(128)}, f32[35,32,32]{2,1,0:T(8,128)S(1)}, f32[35,32]{1,0:T(8,128)S(1)}, s32[]{:T(128)}, ...), condition=%wide.region_5.6_spmd.clone, body=%wide.region_4.5_spmd.clone.sunk | while | flops 110884 | bytes 461563 | solution.py:27
  262.7 1.3 add_select_fusion.9
  397.9 2.4 mul.264
  400.3 3.6 mul.265
  405.8 2.4 reshape.183
  409.1 3.0 fusion.73
  412.2 1.5 reshape.185
  413.7 2.0 fusion.49
  415.7 3.9 reshape.187
  419.5 4.8 multiply_reduce_fusion
  424.4 70.0 %all-reduce.7.cloned.1.call-done = f32[35,32,32]{2,1,0:T(8,128)} async-done(((f32[35,32,32]{2,1,0:T(8,128)}), f32[35,32,32]{2,1,0:T(8,128)}) %all-reduce.7.cloned.1.call-update) | async-done | bytes 143376 | tf_op jit(solution)/shard_map/psum | solution.py:60
  495.4 1.3 collective-permute-start.1
  496.7 4.2 collective-permute-start
  501.0 2.0 select_n.142
  503.1 1.5 fusion.10
  505.7 250.5 %psum.46 = f32[3,3,1120]{2,1,0:T(4,128)S(1)} all-reduce(f32[3,3,1120]{2,1,0:T(4,128)S(1)} %reshape.191), channel_id=1, replica_groups=mesh['tm'=64,'band'=8] {'tm'}, use_global_device_ids=true, to_apply=%region_21.22 | all-reduce | flops 10080 | bytes 80640 | tf_op jit(solution)/shard_map/psum | solution.py:207
  756.2 2.0 reshape.184
  758.2 2.8 convolution_bitcast_fusion.3
  761.0 1.3 copy.49
  762.3 2.5 reshape.186
  764.7 2.2 fusion.4
  768.6 23.9 %all-reduce.1 = (f32[35,32]{1,0:T(8,128)S(1)}, f32[3,3,1120]{2,1,0:T(4,128)S(1)}) all-reduce(f32[35,32]{1,0:T(8,128)S(1)} %reshape.189, f32[3,3,1120]{2,1,0:T(4,128)S(1)} %psum.46), channel_id=1, replica_groups=mesh['tm'=64,'band'=8] {'band'}, use_global_device_ids=true, to_apply=%region_9.10 | all-reduce | flops 11200 | bytes 89600 | tf_op jit(solution)/shard_map/psum | solution.py:60
  792.6 65.7 %all-gather.5 = f32[64,35,32]{1,2,0:T(8,128)} all-gather(f32[1,35,32]{1,2,0:T(8,128)S(1)} %copy.52), channel_id=5, replica_groups=mesh['tm'=64,'band'=8] {'tm'}, dimensions={0}, use_global_device_ids=true | all-gather | bytes 291200 | tf_op jit(solution)/shard_map/all_gather | solution.py:14
  858.9 1.4 fusion.52
  860.3 135.5 %while.35 = (s32[]{:T(128)}, f32[35,32,32]{2,1,0:T(8,128)S(1)}, f32[35,32]{1,0:T(8,128)S(1)}, s32[]{:T(128)}, f32[64,35,32,32]{3,2,1,0:T(8,128)}, /*index=5*/f32...) while((s32[]{:T(128)}, f32[35,32,32]{2,1,0:T(8,128)S(1)}, ...), condition=%wide.region_11.12_spmd.clone, body=%wide.region_10.11_spmd.clone.sunk | while | flops 110888 | bytes 461625 | solution.py:27
  860.3 1.3 add_select_fusion.11
  862.5 1.3 add_select_fusion.11
  864.6 1.3 add_select_fusion.11
  866.7 1.3 add_select_fusion.11
  868.8 1.3 add_select_fusion.11
  873.1 1.3 add_select_fusion.11
  875.2 1.3 add_select_fusion.11
  877.3 1.3 add_select_fusion.11
  879.4 1.3 add_select_fusion.11
  881.5 1.3 add_select_fusion.11
  883.6 1.3 add_select_fusion.11
  887.9 1.3 add_select_fusion.11
  890.0 1.3 add_select_fusion.11
  892.1 1.3 add_select_fusion.11
  894.2 1.3 add_select_fusion.11
  898.5 1.3 add_select_fusion.11
  902.7 1.3 add_select_fusion.11
  904.8 1.3 add_select_fusion.11
  906.9 1.3 add_select_fusion.11
  909.1 1.3 add_select_fusion.11
  913.3 1.3 add_select_fusion.11
  915.4 1.3 add_select_fusion.11
  917.5 1.3 add_select_fusion.11
  919.6 1.3 add_select_fusion.11
  921.8 1.3 add_select_fusion.11
  923.9 1.3 add_select_fusion.11
  928.1 1.3 add_select_fusion.11
  996.0 2.4 mul.306
  998.3 3.6 mul.307
  1003.0 1.5 convolution_bitcast_fusion
  1008.1 1.4 fusion.53
  (592 shorter events, 247.7 us)
Async XLA Ops:
  7.2 1.6 copy-start.18
  7.2 90.1 %all-reduce.5.cloned.1.call-start = ((), (), s32[]{:S(2)}) async-start(), calls=%async_computation | async-start | bytes 1146880 | tf_op jit(solution)/shard_map/psum | solution.py:60
  8.7 1.2 copy-start.5
  9.5 3.0 copy-start.7
  17.3 80.1 %copy-start.3 = (bf16[1,5,26,1120]{3,2,1,0:T(8,128)(2,1)S(1)}, bf16[1,5,26,1120]{3,2,1,0:T(8,128)(2,1)}, u32[]{:S(2)}) copy-start(bf16[1,5,26,1120]{3,2,1,0:T(8,128)(2,1)} %param.12) | copy-start | bytes 873604
  17.3 245.4 %all-gather.9.cloned.1.call-start = ((), (), s32[]{:S(2)}) async-start(), calls=%async_computation.2 | async-start | bytes 37273600 | tf_op jit(solution)/shard_map/all_gather | solution.py:14
  97.3 397.1 %all-reduce.7.cloned.1.call-start = ((), (), s32[]{:S(2)}) async-start(), calls=%async_computation.1 | async-start | bytes 1146880 | tf_op jit(solution)/shard_map/psum | solution.py:60
  98.3 23.0 %copy-start.20 = (bf16[1,5,26,1120]{3,2,1,0:T(8,128)(2,1)S(1)}, bf16[1,5,26,1120]{3,2,1,0:T(8,128)(2,1)}, u32[]{:S(2)}) copy-start(bf16[1,5,26,1120]{3,2,1,0:T(8,128)(2,1)} %param.9) | copy-start | bytes 873604
  123.7 284.6 %copy-start.1 = (f32[130,1120]{1,0:T(8,128)}, f32[130,1120]{1,0:T(8,128)S(1)}, u32[]{:S(2)}) copy-start(f32[130,1120]{1,0:T(8,128)S(1)} %reshape.192) | copy-start | bytes 1747204
  262.7 135.1 %copy-start.16 = (f32[35,32,32]{2,1,0:T(8,128)S(1)}, f32[35,32,32]{2,1,0:T(8,128)}, u32[]{:S(2)}) copy-start(f32[35,32,32]{2,1,0:T(8,128)} %all-reduce.5.cloned.1.call-done) | copy-start | bytes 430084
  400.3 3.6 copy-start.9
  412.2 1.5 copy-start.10
  413.7 5.8 copy-start
  424.3 70.1 %copy-start.17 = (bf16[1,5,26,1120]{3,2,1,0:T(8,128)(2,1)S(1)}, bf16[1,5,26,1120]{3,2,1,0:T(8,128)(2,1)}, u32[]{:S(2)}) copy-start(bf16[1,5,26,1120]{3,2,1,0:T(8,128)(2,1)} %param.11) | copy-start | bytes 873604
  424.4 435.9 %all-gather.11.cloned.1.call-start = ((), (), s32[]{:S(2)}) async-start(), calls=%async_computation.3 | async-start | bytes 37273600 | tf_op jit(solution)/shard_map/all_gather | solution.py:14
  494.5 0.9 copy-start.12
  495.4 7.6 copy-start.21
  495.4 7.7 collective-permute-start.1
  496.7 6.4 collective-permute-start
  762.3 4.6 copy-start.2
  764.7 2.2 copy-start.13
  764.7 2.2 copy-start.14
  767.7 91.2 %copy-start.4 = (f32[5,26,1120]{2,1,0:T(8,128)S(1)}, f32[5,26,1120]{2,1,0:T(8,128)}, u32[]{:S(2)}) copy-start(f32[5,26,1120]{2,1,0:T(8,128)} %reshape.184) | copy-start | bytes 1747204
  860.3 135.6 %copy-start.15 = (f32[35,32,32]{2,1,0:T(8,128)S(1)}, f32[35,32,32]{2,1,0:T(8,128)}, u32[]{:S(2)}) copy-start(f32[35,32,32]{2,1,0:T(8,128)} %all-reduce.7.cloned.1.call-done) | copy-start | bytes 430084
  998.3 3.6 copy-start.6
  1001.9 1.0 copy-start.8
  1004.8 1.1 copy-start.11
  1006.1 1.0 copy-start.19
Sparse Core Ops, SparseCore 0:
  17.5 79.7 all-reduce.4
  100.6 162.1 all-gather.8
  424.5 69.8 all-reduce.6
  497.5 161.5 all-gather.10
